TPU v7x, 32 devices: a whole 2x2x4 slice. The times are simulated.
32 devices in a mesh: blk: 8 (over y, x, core), uly: 4 (over z).
Axes of the slice: x: 2, y: 2, z: 4, core: 2. Of those that a mesh axis runs over, the one named last changes fastest.
Arguments:
- qkv: bfloat16 [2048, 3, 3072], P(('blk', 'uly')), may hold values from -9 to 9
Outputs:
- attended: float32 [2048, 3072], P('blk', 'uly')
- log_total: float32 [24, 2048], P('uly', 'blk')
All inputs are finite; a program needn't handle non-finite values.
Results may differ from a plain program's by a relative error of at most 0.0027.
Values may be sent and summed in bfloat16 or wider, within the bound.
No kernel may reach another device: no remote copies, remote signals or barrier semaphores. Data moves between devices by JAX's collectives and lax.ppermute only.
A program may use at most 64 MiB of HBM per device.

v0:
```python
import math
import jax
import jax.numpy as jnp
from jax import lax
from jax.sharding import PartitionSpec as P

HEAD_DIM = 128


def from_behind(value, axis, steps):
    count = lax.axis_size(axis)
    pairs = [(source, (source + steps) % count) for source in range(count)]
    return lax.ppermute(value, axis, pairs)


def block_scores(query_rows, key_rows, temper):
    return (
        jnp.einsum("rhd,khd->hrk", query_rows, key_rows, preferred_element_type=jnp.float32)
        * temper
    )


def attend_first(query_rows, key_rows, value_rows, temper):
    scores = block_scores(query_rows, key_rows, temper)
    top = jnp.max(scores, axis=2)
    weights = jnp.exp(scores - top[:, :, None])
    total = jnp.sum(weights, axis=2)
    accum = jnp.einsum(
        "hrk,khd->hrd", weights.astype(jnp.bfloat16), value_rows, preferred_element_type=jnp.float32
    )
    return (top, total, accum)


def attend_next(running, query_rows, key_rows, value_rows, temper):
    top, total, accum = running
    scores = block_scores(query_rows, key_rows, temper)
    newtop = jnp.maximum(top, jnp.max(scores, axis=2))
    factor = jnp.exp(top - newtop)
    weights = jnp.exp(scores - newtop[:, :, None])
    total = total * factor + jnp.sum(weights, axis=2)
    accum = accum * factor[:, :, None] + jnp.einsum(
        "hrk,khd->hrd", weights.astype(jnp.bfloat16), value_rows, preferred_element_type=jnp.float32
    )
    return (newtop, total, accum)


def shards(qkv):
    width = qkv.shape[2] // lax.axis_size("uly")
    heads_local = width // HEAD_DIM
    temper = 1.0 / math.sqrt(HEAD_DIM)
    grouped = lax.all_to_all(qkv, "uly", split_axis=2, concat_axis=0, tiled=True)
    prev_pairs = from_behind(grouped[:, 1:], "blk", 1)
    block_len = grouped.shape[0]
    row_count = math.gcd(block_len, 512)
    queries = grouped[:, 0].reshape(block_len // row_count, row_count, heads_local, HEAD_DIM)
    own_keys = grouped[:, 1].reshape(block_len, heads_local, HEAD_DIM)
    own_values = grouped[:, 2].reshape(block_len, heads_local, HEAD_DIM)
    prev_keys = prev_pairs[:, 0].reshape(block_len, heads_local, HEAD_DIM)
    prev_values = prev_pairs[:, 1].reshape(block_len, heads_local, HEAD_DIM)

    def per_rows(query_rows):
        running = attend_first(query_rows, own_keys, own_values, temper)
        top, total, accum = attend_next(running, query_rows, prev_keys, prev_values, temper)
        normed = accum / total[:, :, None]
        return (jnp.transpose(normed, (1, 0, 2)).reshape(row_count, width), top + jnp.log(total))

    attended_rows, log_rows = lax.map(per_rows, queries)
    attended = attended_rows.reshape(block_len, width)
    log_total = jnp.transpose(log_rows, (1, 0, 2)).reshape(heads_local, block_len)
    return (attended, log_total)


def solution(mesh):
    placed = (P(("blk", "uly"), None, None),)
    return jax.shard_map(
        shards,
        mesh=mesh,
        in_specs=placed,
        out_specs=(P("blk", "uly"), P("uly", "blk")),
        check_vma=False,
    )
```

profile of v0, /device:TPU:0, one launch (start us, length us, event | category | flops | bytes accessed | tf_op | source)
XLA Modules:
  0.0 74.6 jit_solution(17815620228269308837)
XLA Ops:
  0.6 4.6 %copy.32 = bf16[64,3,3072]{0,1,2:T(4,128)(2,1)S(1)} copy(bf16[64,3,3072]{2,0,1:T(8,128)(2,1)} %param.1) | data formatting | bytes 2359296 | tf_op args[0]
  5.2 3.1 %reshape.40 = bf16[4,2,73728]{2,1,0:T(2,128)(2,1)} reshape(bf16[3072,3,64]{2,1,0:T(4,128)(2,1)S(1)} %bitcast.42) | data formatting | bytes 2359296
  8.3 35.0 %all_to_all.18 = bf16[4,2,73728]{2,1,0:T(2,128)(2,1)} all-to-all(bf16[4,2,73728]{2,1,0:T(2,128)(2,1)} %reshape.40), channel_id=1, replica_groups=mesh['blk'=8,'uly'=4] {'uly'}, dimensions={0} | all-to-all | bytes 2359296 | tf_op jit(solution)/shard_map/all_to_all | solution.py:51
  43.2 3.5 %reshape.41 = bf16[3072,3,64]{2,1,0:T(4,128)(2,1)S(1)} reshape(bf16[4,2,73728]{2,1,0:T(2,128)(2,1)} %all_to_all.18) | data formatting | bytes 2359296
  46.7 3.2 %copy.34 = bf16[4,64,3,768]{3,1,0,2:T(8,128)(2,1)} copy(bf16[4,64,3,768]{1,2,3,0:T(4,128)(2,1)S(1)} %bitcast.41) | data formatting | bytes 2359296 | tf_op jit(solution)/shard_map/all_to_all | solution.py:51
  49.9 2.2 %slice.27 = bf16[256,2,768]{2,0,1:T(8,128)(2,1)} slice(bf16[256,3,768]{2,0,1:T(8,128)(2,1)} %bitcast.43), slice={[0:256], [1:3], [0:768]} | slice | bytes 1572864 | tf_op jit(solution)/shard_map/slice | solution.py:52
  52.1 0.0 collective-permute-start
  52.1 0.1 fusion.13
  52.2 0.2 copy.36
  52.3 0.9 %copy.39 = bf16[256,1,768]{0,2,1:T(8,128)(2,1)} copy(bf16[256,1,768]{2,0,1:T(8,128)(2,1)S(1)} %get-tuple-element.37) | data formatting | bytes 786432 | tf_op jit(solution)/shard_map/slice | solution.py:57
  53.2 0.2 copy.35
  53.4 0.4 fusion.15
  53.8 10.9 %collective-permute-done = bf16[256,2,768]{2,0,1:T(8,128)(2,1)} collective-permute-done((bf16[256,2,768]{2,0,1:T(8,128)(2,1)}, bf16[256,2,768]{2,0,1:T(8,128)(2,1)}, u32[]{:S(2)}, u32[]{:S(2)}) %collective-permute-start) | collective-permute-done | bytes 786464 | tf_op jit(solution)/shard_map/ppermute | solution.py:13
  64.7 1.9 %fusion.14 = (bf16[256,1,768]{2,0,1:T(8,128)(2,1)}, bf16[256,1,768]{2,0,1:T(8,128)(2,1)S(1)}) fusion(bf16[256,2,768]{2,0,1:T(8,128)(2,1)} %collective-permute-done), kind=kLoop, calls=%fused_computation.21 | loop fusion | bytes 1572864 | tf_op jit(solution)/shard_map/slice | solution.py:59
  66.6 0.9 %copy.41 = bf16[256,1,768]{0,2,1:T(8,128)(2,1)} copy(bf16[256,1,768]{2,0,1:T(8,128)(2,1)S(1)} %get-tuple-element.40) | data formatting | bytes 786432 | tf_op jit(solution)/shard_map/slice | solution.py:58
  67.5 1.4 %fusion.16 = (f32[6,256]{1,0:T(8,128)S(1)}, f32[6,256,256]{1,2,0:T(8,128)S(1)}) fusion(bf16[256,6,128]{0,2,1:T(8,128)(2,1)S(1)} %bitcast.46, bf16[256,6,128]{0,2,1:T(8,128)(2,1)} %bitcast.48), kind=kOutput, calls=%fused_computation.23 | convolution fusion | flops 101448192 | bytes 2365440 | tf_op jit(solution)/shard_map/while/body/eval_jaxpr/rhd,khd->hrk/dot_general | solution.py:18
  69.0 0.0 copy-start.1
  69.0 0.4 fusion
  69.4 0.6 log_add_fusion
  70.0 0.6 bitcast_add_fusion
  70.7 0.9 %copy.44 = bf16[256,1,768]{0,2,1:T(8,128)(2,1)} copy(bf16[256,1,768]{2,0,1:T(8,128)(2,1)S(1)} %copy-done.1) | data formatting | bytes 786432 | tf_op jit(solution)/shard_map/slice | solution.py:59
  71.6 1.5 %fusion.4 = f32[256,6,128]{0,2,1:T(8,128)S(1)} fusion(bf16[256,6,128]{0,2,1:T(8,128)(2,1)} %bitcast.49, f32[6,256,256]{1,2,0:T(8,128)S(1)} %get-tuple-element.42, f32[6,256]{1,0:T(8,128)S(1)} %get-tuple-element.41, f32[256,6]{0,1:T(8,128)} %get-tuple-element.35), kind=kOutput, calls=%fused_computation.10 | convolution fusion | flops 101646336 | bytes 2764800 | tf_op jit(solution)/shard_map/while/body/eval_jaxpr/hrk,khd->hrd/dot_general | solution.py:28
  73.1 0.4 fusion.6
  73.5 1.1 %copy.46 = f32[256,768]{1,0:T(8,128)} copy(f32[256,768]{0,1:T(8,128)S(1)} %bitcast.50) | data formatting | bytes 1572864
  (8 shorter events, 0.0 us)
Async XLA Ops:
  49.9 2.2 %copy-start = (bf16[4,64,3,768]{3,1,0,2:T(8,128)(2,1)S(1)}, bf16[4,64,3,768]{3,1,0,2:T(8,128)(2,1)}, u32[]{:S(2)}) copy-start(bf16[4,64,3,768]{3,1,0,2:T(8,128)(2,1)} %copy.34) | copy-start | bytes 3538948
  52.1 12.6 %collective-permute-start = (bf16[256,2,768]{2,0,1:T(8,128)(2,1)}, bf16[256,2,768]{2,0,1:T(8,128)(2,1)}, u32[]{:S(2)}, u32[]{:S(2)}) collective-permute-start(bf16[256,2,768]{2,0,1:T(8,128)(2,1)} %slice.27), channel_id=1, source_target_pairs={{0,4},{4,8},{8,12},{12,16},{16,20},{20,24},{24,28},{28,0},{1,5},{5... | collective-permute-start | bytes 2359304 | tf_op jit(solution)/shard_map/ppermute | solution.py:13
  69.0 1.7 %copy-start.1 = (bf16[256,1,768]{2,0,1:T(8,128)(2,1)S(1)}, bf16[256,1,768]{2,0,1:T(8,128)(2,1)}, u32[]{:S(2)}) copy-start(bf16[256,1,768]{2,0,1:T(8,128)(2,1)} %get-tuple-element.39) | copy-start | bytes 1179652
  71.6 1.5 %copy-start.2 = (bf16[256,1,768]{0,2,1:T(8,128)(2,1)S(1)}, bf16[256,1,768]{0,2,1:T(8,128)(2,1)}, u32[]{:S(2)}) copy-start(bf16[256,1,768]{0,2,1:T(8,128)(2,1)} %copy.44) | copy-start | bytes 1179652
  71.6 1.5 %copy-start.3 = (f32[256,6]{0,1:T(8,128)S(1)}, f32[256,6]{0,1:T(8,128)}, u32[]{:S(2)}) copy-start(f32[256,6]{0,1:T(8,128)} %get-tuple-element.34) | copy-start | bytes 18436
where the time goes:
time: 75 us; the launch traced here: 74.6 us
  blocking collectives  35 us (47%)
  local copies, waits for them, and re-layouts  22.7 us (30%)
  waiting for transfers between devices  10.9 us (15%)
  matrix products  3.71 us (5%)
  other arithmetic  1.68 us (2%)
    all_to_all x1, blocking collectives, shards(): lax.all_to_all(qkv, 'uly', split_axis=2, concat_axis=0, tiled=True)  35 us
    unnamed x12, local copies, waits for them, and re-layouts  12.3 us
    ppermute x1, waiting for transfers between devices, from_behind(): return lax.ppermute(value, axis, pairs)  10.9 us
    all_to_all x1, local copies, waits for them, and re-layouts, shards(): lax.all_to_all(qkv, 'uly', split_axis=2, concat_axis=0, tiled=True)  3.21 us
    slice x2, local copies, waits for them, and re-layouts, shards(): prev_values = prev_pairs[:, 1].reshape(block_len, heads_local, HEAD_DIM)  2.83 us
    slice x1, local copies, waits for them, and re-layouts, shards(): prev_pairs = from_behind(grouped[:, 1:], 'blk', 1)  2.16 us
    dot_general x2, matrix products, block_scores(): jnp.einsum('rhd,khd->hrk', query_rows, key_rows, preferred_element_type=j...  1.84 us
  transfers between devices with their start and end apart: 1, of which 1 were waited for; matrix products, arithmetic and copies ran while one was open for 2% of the time, Pallas kernels for 0%

commit v1 on v0

--- a/solution.py
+++ b/solution.py
@@ -5,6 +5,18 @@
 from jax.sharding import PartitionSpec as P
 
 HEAD_DIM = 128
+
+
+def rotated_exchange(x, axis, split, join):
+    ways, here = (lax.axis_size(axis), lax.axis_index(axis))
+    width = x.shape[split] // ways
+    turned = jnp.roll(x, -here * width, axis=split)
+    got = [lax.slice_in_dim(turned, 0, width, axis=split)]
+    for far in range(1, ways):
+        sent = lax.slice_in_dim(turned, far * width, (far + 1) * width, axis=split)
+        got.append(lax.ppermute(sent, axis, [(d, (d + far) % ways) for d in range(ways)]))
+    line = jnp.concatenate(got[::-1], axis=join)
+    return jnp.roll(line, (here + 1) * got[0].shape[join], axis=join)
 
 
 def from_behind(value, axis, steps):
@@ -48,7 +60,7 @@
     width = qkv.shape[2] // lax.axis_size("uly")
     heads_local = width // HEAD_DIM
     temper = 1.0 / math.sqrt(HEAD_DIM)
-    grouped = lax.all_to_all(qkv, "uly", split_axis=2, concat_axis=0, tiled=True)
+    grouped = rotated_exchange(qkv, "uly", 2, 0)
     prev_pairs = from_behind(grouped[:, 1:], "blk", 1)
     block_len = grouped.shape[0]
     row_count = math.gcd(block_len, 512)

time: 75 us -> 62.8 us (0.84)
  blocking collectives: 35 us -> 0 us
  waiting for transfers between devices: 10.9 us -> 34.8 us
  local copies, waits for them, and re-layouts: 22.7 us -> 14.9 us
  starting transfers between devices: 0.01 us -> 6.23 us
  other arithmetic: 1.68 us -> 4.07 us
  matrix products: 3.71 us -> 1.67 us
    all_to_all x1 -> x0, blocking collectives: 35 us -> none  [shards(): lax.all_to_all(qkv, 'uly', split_axis=2, concat_axis=0, tiled=True)]
    ppermute x0 -> x3, waiting for transfers between devices: none -> 23.2 us  [rotated_exchange(): lax.ppermute(sent, axis, [(d, (d + far) % ways) for d in range(ways)])]
    unnamed x12 -> x2, local copies, waits for them, and re-layouts: 12.3 us -> 3.92 us
    ppermute x0 -> x3, starting transfers between devices: none -> 6.22 us  [rotated_exchange(): lax.ppermute(sent, axis, [(d, (d + far) % ways) for d in range(ways)])]
    concatenate x0 -> x1, local copies, waits for them, and re-layouts: none -> 5.95 us  [rotated_exchange(): return jnp.roll(line, (here + 1) * got[0].shape[join], axis=join)]
    all_to_all x1 -> x0, local copies, waits for them, and re-layouts: 3.21 us -> none  [shards(): lax.all_to_all(qkv, 'uly', split_axis=2, concat_axis=0, tiled=True)]
    concatenate x0 -> x1, other arithmetic: none -> 2.99 us  [rotated_exchange(): turned = jnp.roll(x, -here * width, axis=split)]
    ppermute x0 -> x3, local copies, waits for them, and re-layouts: none -> 2.43 us  [rotated_exchange(): lax.ppermute(sent, axis, [(d, (d + far) % ways) for d in range(ways)])]
  transfers between devices with their start and end apart: 1 -> 4, of which waited for: 1 -> 3; matrix products, arithmetic and copies ran while one was open for 2% -> 4% of each run, Pallas kernels for 0% -> 0%
where the time goes in v1:
time: 62.8 us; the launch traced here: 62.4 us
  waiting for transfers between devices  34.8 us (55%)
  local copies, waits for them, and re-layouts  14.9 us (24%)
  starting transfers between devices  6.23 us (10%)
  other arithmetic  4.07 us (6%)
  matrix products  1.67 us (3%)
  between operations  0.78 us (1%)
    ppermute x3, waiting for transfers between devices, rotated_exchange(): lax.ppermute(sent, axis, [(d, (d + far) % ways) for d in range(ways)])  23.2 us
    ppermute x1, waiting for transfers between devices, from_behind(): return lax.ppermute(value, axis, pairs)  11.6 us
    ppermute x3, starting transfers between devices, rotated_exchange(): lax.ppermute(sent, axis, [(d, (d + far) % ways) for d in range(ways)])  6.22 us
    concatenate x1, local copies, waits for them, and re-layouts, rotated_exchange(): return jnp.roll(line, (here + 1) * got[0].shape[join], axis=join)  5.95 us
    unnamed x2, local copies, waits for them, and re-layouts  3.92 us
    concatenate x1, other arithmetic, rotated_exchange(): turned = jnp.roll(x, -here * width, axis=split)  2.99 us
    ppermute x3, local copies, waits for them, and re-layouts, rotated_exchange(): lax.ppermute(sent, axis, [(d, (d + far) % ways) for d in range(ways)])  2.43 us
  transfers between devices with their start and end apart: 4, of which 3 were waited for; matrix products, arithmetic and copies ran while one was open for 4% of the time, Pallas kernels for 0%

profile of v1, /device:TPU:0, one launch (start us, length us, event | category | flops | bytes accessed | tf_op | source)
XLA Modules:
  0.0 62.4 jit_solution(17585784282270770420)
XLA Ops:
  0.7 2.8 %copy.17 = bf16[64,3,3072]{0,2,1:T(8,128)(2,1)S(1)} copy(bf16[64,3,3072]{2,0,1:T(8,128)(2,1)} %param.1) | data formatting | bytes 2359296 | tf_op args[0]
  3.4 3.0 %fusion = bf16[64,3,3072]{0,2,1:T(8,128)(2,1)S(1)} fusion(s32[]{:T(128)S(6)} %select_n.24, bf16[64,3,3072]{0,2,1:T(8,128)(2,1)S(1)} %copy.17), kind=kLoop, calls=%fused_computation.2 | loop fusion | flops 2359296 | bytes 2359300 | tf_op jit(solution)/shard_map/jit(_roll_dynamic)/concatenate | solution.py:13
  6.4 0.2 fusion.14
  6.6 0.2 copy.19
  6.8 5.1 %collective-permute-start = (bf16[64,3,768]{2,0,1:T(8,128)(2,1)S(1)}, bf16[64,3,768]{2,0,1:T(8,128)(2,1)S(1)}, u32[]{:S(2)}, u32[]{:S(2)}) collective-permute-start(bf16[64,3,768]{2,0,1:T(8,128)(2,1)S(1)} %copy.19), channel_id=1, source_target_pairs={{0,3},{1,0},{2,1},{3,2},{4,7},{5,4},{6,5},{7,6},{8,11},{9,8},{10,9... | collective-permute-start | bytes 884744 | tf_op jit(solution)/shard_map/ppermute | solution.py:17
  11.9 0.2 copy.20
  12.2 0.2 copy.21
  12.5 1.1 %collective-permute-start.2 = (bf16[64,3,768]{2,0,1:T(8,128)(2,1)S(1)}, bf16[64,3,768]{2,0,1:T(8,128)(2,1)S(1)}, u32[]{:S(2)}, u32[]{:S(2)}) collective-permute-start(bf16[64,3,768]{2,0,1:T(8,128)(2,1)S(1)} %copy.21), channel_id=1, source_target_pairs={{0,1},{1,2},{2,3},{3,0},{4,5},{5,6},{6,7},{7,4},{8,9},{9,10},{10,1... | collective-permute-start | bytes 884744 | tf_op jit(solution)/shard_map/ppermute | solution.py:17
  13.5 5.9 %collective-permute-done = bf16[64,3,768]{2,0,1:T(8,128)(2,1)S(1)} collective-permute-done((bf16[64,3,768]{2,0,1:T(8,128)(2,1)S(1)}, bf16[64,3,768]{2,0,1:T(8,128)(2,1)S(1)}, u32[]{:S(2)}, u32[]{:S(2)}) %collective-permute-start) | collective-permute-done | bytes 294944 | tf_op jit(solution)/shard_map/ppermute | solution.py:17
  19.4 0.3 copy.22
  19.7 17.3 %collective-permute-done.1 = bf16[64,3,768]{2,0,1:T(8,128)(2,1)S(1)} collective-permute-done((bf16[64,3,768]{2,0,1:T(8,128)(2,1)S(1)}, bf16[64,3,768]{2,0,1:T(8,128)(2,1)S(1)}, u32[]{:S(2)}, u32[]{:S(2)}) %collective-permute-start.1) | collective-permute-done | bytes 294944 | tf_op jit(solution)/shard_map/ppermute | solution.py:17
  37.1 1.1 %copy.23 = bf16[64,3,768]{0,2,1:T(8,128)(2,1)} copy(bf16[64,3,768]{2,0,1:T(8,128)(2,1)S(1)} %collective-permute-done.1) | data formatting | bytes 589824 | tf_op jit(solution)/shard_map/ppermute | solution.py:17
  38.1 1.1 %copy.24 = bf16[64,3,768]{0,2,1:T(8,128)(2,1)} copy(bf16[64,3,768]{2,0,1:T(8,128)(2,1)S(1)} %collective-permute-done.2) | data formatting | bytes 589824 | tf_op jit(solution)/shard_map/ppermute | solution.py:17
  39.2 5.9 %concatenate.11 = bf16[512,3,768]{0,2,1:T(8,128)(2,1)S(1)} concatenate(bf16[64,3,768]{0,2,1:T(8,128)(2,1)S(1)} %copy.22, bf16[64,3,768]{0,2,1:T(8,128)(2,1)} %copy.23, bf16[64,3,768]{0,2,1:T(8,128)(2,1)} %copy.24, bf16[64,3,768]{0,2,1:T(8,128)(2,1)S(1)} %get-tuple-element.37, bf16[64,3,768]{0,2,1:T(8,128)(2,1)S(1)} %copy.22, bf16[64,3,768]{0,2,1:T(8,128)(2,1)} %copy.23, ...), dimensions={0} | concatenate | bytes 4718592 | tf_op jit(solution)/shard_map/jit(_roll_dynamic)/concatenate | solution.py:19
  45.1 1.2 %constant_dynamic-slice_fusion.2 = bf16[256,2,768]{0,2,1:T(8,128)(2,1)} fusion(bf16[512,3,768]{0,2,1:T(8,128)(2,1)S(1)} %concatenate.11, s32[]{:T(128)S(6)} %select_n.26, s32[]{:T(128)S(6)} %add.56), kind=kLoop, calls=%fused_computation.25 | loop fusion | bytes 1572872 | tf_op jit(solution)/shard_map/slice | solution.py:64
  46.3 0.5 constant_dynamic-slice_fusion.1
  46.8 0.4 fusion.16
  47.2 11.6 %collective-permute-done.3 = bf16[256,2,768]{0,2,1:T(8,128)(2,1)S(1)} collective-permute-done((bf16[256,2,768]{0,2,1:T(8,128)(2,1)}, bf16[256,2,768]{0,2,1:T(8,128)(2,1)S(1)}, u32[]{:S(2)}, u32[]{:S(2)}) %collective-permute-start.3) | collective-permute-done | bytes 786464 | tf_op jit(solution)/shard_map/ppermute | solution.py:25
  58.9 0.4 fusion.17
  59.4 0.4 fusion.1
  59.8 0.6 log_add_fusion
  60.4 0.4 convolution_bitcast_fusion
  60.9 0.4 fusion.7
  61.3 1.1 %copy.34 = f32[256,768]{1,0:T(8,128)} copy(f32[256,768]{0,1:T(8,128)S(1)} %bitcast.39) | data formatting | bytes 1572864
  (6 shorter events, 0.1 us)
Async XLA Ops:
  6.8 12.6 %collective-permute-start = (bf16[64,3,768]{2,0,1:T(8,128)(2,1)S(1)}, bf16[64,3,768]{2,0,1:T(8,128)(2,1)S(1)}, u32[]{:S(2)}, u32[]{:S(2)}) collective-permute-start(bf16[64,3,768]{2,0,1:T(8,128)(2,1)S(1)} %copy.19), channel_id=1, source_target_pairs={{0,3},{1,0},{2,1},{3,2},{4,7},{5,4},{6,5},{7,6},{8,11},{9,8},{10,9... | collective-permute-start | bytes 884744 | tf_op jit(solution)/shard_map/ppermute | solution.py:17
  12.2 24.9 %collective-permute-start.1 = (bf16[64,3,768]{2,0,1:T(8,128)(2,1)S(1)}, bf16[64,3,768]{2,0,1:T(8,128)(2,1)S(1)}, u32[]{:S(2)}, u32[]{:S(2)}) collective-permute-start(bf16[64,3,768]{2,0,1:T(8,128)(2,1)S(1)} %copy.20), channel_id=1, source_target_pairs={{0,2},{1,3},{2,0},{3,1},{4,6},{5,7},{6,4},{7,5},{8,10},{9,11},{10,... | collective-permute-start | bytes 884744 | tf_op jit(solution)/shard_map/ppermute | solution.py:17
  12.5 25.6 %collective-permute-start.2 = (bf16[64,3,768]{2,0,1:T(8,128)(2,1)S(1)}, bf16[64,3,768]{2,0,1:T(8,128)(2,1)S(1)}, u32[]{:S(2)}, u32[]{:S(2)}) collective-permute-start(bf16[64,3,768]{2,0,1:T(8,128)(2,1)S(1)} %copy.21), channel_id=1, source_target_pairs={{0,1},{1,2},{2,3},{3,0},{4,5},{5,6},{6,7},{7,4},{8,9},{9,10},{10,1... | collective-permute-start | bytes 884744 | tf_op jit(solution)/shard_map/ppermute | solution.py:17
  46.3 12.5 %collective-permute-start.3 = (bf16[256,2,768]{0,2,1:T(8,128)(2,1)}, bf16[256,2,768]{0,2,1:T(8,128)(2,1)S(1)}, u32[]{:S(2)}, u32[]{:S(2)}) collective-permute-start(bf16[256,2,768]{0,2,1:T(8,128)(2,1)} %constant_dynamic-slice_fusion.2), channel_id=1, source_target_pairs={{0,4},{4,8},{8,12},{12,16},{16,20},{20,24},{24,28},{28,0},{1,5},{5... | collective-permute-start | bytes 2359304 | tf_op jit(solution)/shard_map/ppermute | solution.py:25
